TPU v7x, 32 devices: a whole 2x2x4 slice. The times are simulated.
32 devices in a mesh: dp: 4 (over y, x), expert: 4 (over z), tensor: 2 (over core).
Axes of the slice: x: 2, y: 2, z: 4, core: 2. Of those that a mesh axis runs over, the one named last changes fastest.
Arguments:
- tokens: bfloat16 [2048, 2048], P(('dp', 'expert'), 'tensor'), may hold values from -6 to 6
- norm_gain: bfloat16 [2048], replicated, may hold values from 0.25 to 1.75
- expert_ids: int32 [2048, 2], P(('dp', 'expert')), may hold values from 0 to 3, all different within a row; in each aligned block of 128 rows (0 to 127, 128 to 255, ...) at most 128 rows name the same one
- gate_codes: int32 [2048, 2], P(('dp', 'expert')), may hold values from 1 to 255
- gate_weights: bfloat16 [4, 7168, 2048], P('expert', ('dp', 'tensor')), may hold values from -0.125 to 0.125
- up_weights: bfloat16 [4, 7168, 2048], P('expert', ('dp', 'tensor')), may hold values from -0.125 to 0.125
- down_weights: bfloat16 [4, 7168, 2048], P('expert', ('dp', 'tensor')), may hold values from -0.0625 to 0.0625
- value_head: bfloat16 [2048, 128], replicated, may hold values from -0.125 to 0.125
- actions: int32 [2048], P(('dp', 'expert')), may hold values from 0 to 127
- rewards: int32 [2048], P(('dp', 'expert')), may hold values from -8 to 8
- trace_codes: int32 [2048], P(('dp', 'expert')), may hold values from 1 to 1024
Outputs:
- action_values: float32 [2048, 128], P(('dp', 'expert'))
- retrace_targets: float32 [2048], P(('dp', 'expert'))
Inputs may be any that keep to these rules, and one draw needn't show every extreme that they name: `expert_ids`: each row names 2 different experts; within the 128 rows of one index pair of dp and expert each expert is named by at most 128 rows, and in some of these blocks one expert by exactly 128.
All inputs are finite; a program needn't handle non-finite values.
Results may differ from a plain program's by a relative error of at most 0.005.
Values may be sent and summed in bfloat16 or wider, within the bound.
No kernel may reach another device: no remote copies, remote signals or barrier semaphores. Data moves between devices by JAX's collectives and lax.ppermute only.
A program may use at most 256 MiB of HBM per device.

v0:
```python
import jax
import jax.numpy as jnp
from jax import lax
from jax.sharding import PartitionSpec as P

TOP = 2
STEPS = 128
DISCOUNT = 0.99
EPSILON = 1e-05


def expert_rows(row_block, gate_matrix, lift_matrix, down_matrix):
    gate_value = lax.dot_general(
        row_block, gate_matrix, (((1,), (1,)), ((), ())), preferred_element_type=jnp.float32
    )
    lift_value = lax.dot_general(
        row_block, lift_matrix, (((1,), (1,)), ((), ())), preferred_element_type=jnp.float32
    )
    hidden = (jax.nn.silu(gate_value) * lift_value).astype(jnp.bfloat16)
    return jnp.dot(hidden, down_matrix, preferred_element_type=jnp.float32)


def retrace(action_values, actions, rewards, trace_codes):
    greedy = jnp.max(action_values, axis=1)
    picked = (
        actions[:, None] == jnp.arange(action_values.shape[1], dtype=jnp.int32)[None, :]
    ).astype(jnp.float32)
    taken = jnp.sum(action_values * picked, axis=1)
    trace = trace_codes.astype(jnp.float32) / 1024.0
    reward = rewards.astype(jnp.float32) * 0.25
    greedy = greedy.reshape(-1, STEPS)
    taken = taken.reshape(-1, STEPS)
    trace = trace.reshape(-1, STEPS)
    reward = reward.reshape(-1, STEPS)
    padding = jnp.zeros_like(greedy[:, :1])
    greedy_next = jnp.concatenate([greedy[:, 1:], padding], axis=1)
    taken_next = jnp.concatenate([taken[:, 1:], padding], axis=1)
    trace_next = jnp.concatenate([trace[:, 1:], padding], axis=1)
    driver = reward + DISCOUNT * (greedy_next - trace_next * taken_next)
    log_sums = jnp.cumsum(jnp.log(DISCOUNT * trace), axis=1)
    spans = log_sums[:, None, :] - log_sums[:, :, None]
    upper_mask = (
        jnp.arange(STEPS, dtype=jnp.int32)[None, :] >= jnp.arange(STEPS, dtype=jnp.int32)[:, None]
    )
    weight = jnp.where(upper_mask[None, :, :], jnp.exp(jnp.minimum(spans, 0.0)), 0.0)
    target = jnp.einsum("nts,ns->nt", weight, driver, precision=lax.Precision.HIGHEST)
    return target.reshape(-1)


def per_device(
    tokens,
    norm_gain,
    expert_ids,
    gate_codes,
    gate_weights,
    up_weights,
    down_weights,
    value_head,
    actions,
    rewards,
    trace_codes,
):
    groups = lax.axis_size("expert")
    tok_rows = tokens.shape[0]
    capacity = 2 * tok_rows * TOP // groups
    head_wide = value_head.astype(jnp.float32)
    flat_ids = expert_ids.reshape(-1)
    marked = (flat_ids[:, None] == jnp.arange(groups, dtype=jnp.int32)[None, :]).astype(jnp.int32)
    places = jnp.sum((jnp.cumsum(marked, axis=0) - 1) * marked, axis=1)
    slot_of = (flat_ids * capacity + places).reshape(tok_rows, TOP)
    slot_range = jnp.arange(groups * capacity, dtype=jnp.int32)
    matches = slot_of[None, :, :] == slot_range[:, None, None]
    dispatch_map = jnp.any(matches, axis=2).astype(jnp.bfloat16)
    outgoing = jnp.dot(dispatch_map, tokens, preferred_element_type=jnp.float32).astype(
        jnp.bfloat16
    )
    outgoing = outgoing.reshape(groups, capacity, tokens.shape[1])
    arrived = lax.all_to_all(outgoing, "expert", split_axis=0, concat_axis=0, tiled=True)
    arrived = lax.all_gather(arrived, "tensor", axis=2, tiled=True)
    row_count = groups * capacity
    row_block = arrived.reshape(row_count, arrived.shape[2])
    widened = row_block.astype(jnp.float32)
    scaling = lax.rsqrt(jnp.mean(widened * widened, axis=1, keepdims=True) + EPSILON)
    normed = (widened * scaling * norm_gain.astype(jnp.float32)[None, :]).astype(jnp.bfloat16)
    gathered = lax.all_gather(normed, "dp", axis=0, tiled=True)
    payload = lax.psum_scatter(
        expert_rows(gathered, gate_weights[0], up_weights[0], down_weights[0]),
        "dp",
        scatter_dimension=0,
        tiled=True,
    )
    returned = lax.all_to_all(
        payload.reshape(groups, capacity, payload.shape[1]),
        "expert",
        split_axis=0,
        concat_axis=0,
        tiled=True,
    )
    returned = returned.reshape(row_count, payload.shape[1])
    codes = gate_codes.astype(jnp.float32)
    gate_share = codes / jnp.sum(codes, axis=1, keepdims=True)
    combine_map = jnp.sum(jnp.where(matches, gate_share[None, :, :], 0.0), axis=2)
    blended = lax.dot_general(
        combine_map,
        returned,
        (((0,), (0,)), ((), ())),
        precision=lax.Precision.HIGHEST,
        preferred_element_type=jnp.float32,
    )
    partial_values = jnp.dot(
        blended, head_wide, precision=lax.Precision.HIGHEST, preferred_element_type=jnp.float32
    )
    action_values = lax.psum(partial_values, "tensor")
    retrace_targets = retrace(action_values, actions, rewards, trace_codes)
    return (action_values, retrace_targets)


def solution(mesh):
    in_specs = (
        P(("dp", "expert"), "tensor"),
        P(),
        P(("dp", "expert"), None),
        P(("dp", "expert"), None),
        P("expert", ("dp", "tensor"), None),
        P("expert", ("dp", "tensor"), None),
        P("expert", ("dp", "tensor"), None),
        P(),
        P(("dp", "expert")),
        P(("dp", "expert")),
        P(("dp", "expert")),
    )
    out_specs = (P(("dp", "expert"), None), P(("dp", "expert")))
    return jax.shard_map(
        per_device, mesh=mesh, in_specs=in_specs, out_specs=out_specs, check_vma=False
    )
```

profile of v0, /device:TPU:0, one launch (start us, length us, event | category | flops | bytes accessed | tf_op | source)
XLA Modules:
  0.0 473.5 jit_solution(6893080322555966808)
XLA Ops:
  7.2 0.0 copy-start
  7.2 0.0 copy-start.1
  7.2 0.0 all-gather.3.cloned.1.call-start
  7.2 0.8 copy.34
  8.1 0.1 eq.53
  8.2 0.1 eq.49
  8.4 1.2 reduce-window.14
  9.6 0.1 slice.20
  9.7 0.1 copy.36
  9.8 0.1 copy.37
  9.9 0.1 add_bitcast_fusion
  10.0 0.1 reduce_sum.48
  10.2 0.1 copy.38
  10.2 0.7 multiply_add_fusion
  10.9 0.1 fusion.9
  11.0 1.4 convolution_convert_fusion
  12.4 32.0 %all_to_all.10 = bf16[4,128,1024]{2,1,0:T(8,128)(2,1)} all-to-all(bf16[4,128,1024]{2,1,0:T(8,128)(2,1)S(1)} %bitcast.62), channel_id=1, replica_groups=mesh['dp'=4,'expert'=4,'tensor'=2] {'expert'}, dimensions={0} | all-to-all | bytes 2097152 | tf_op jit(solution)/shard_map/all_to_all | solution.py:78
  44.3 0.0 all-gather.3.cloned.1.call-update
  44.4 0.0 all-gather.5.cloned.1.call-start
  44.4 0.0 copy-done.1
  44.4 9.8 %all-gather.3.cloned.1.call-done = bf16[4,128,2048]{2,1,0:T(8,128)(2,1)} async-done(((bf16[4,128,1024]{2,1,0:T(8,128)(2,1)}), bf16[4,128,2048]{2,1,0:T(8,128)(2,1)}) %all-gather.3.cloned.1.call-update) | async-done | bytes 2097168 | tf_op jit(solution)/shard_map/all_gather | solution.py:79
  54.2 2.1 multiply_reduce_fusion
  56.3 3.4 fusion.1
  59.7 0.0 all-gather.5.cloned.1.call-update
  59.7 0.2 reduce-scatter.2.cloned.1.call-start
  60.0 88.6 %all-gather.5.cloned.1.call-done = bf16[2048,2048]{1,0:T(8,128)(2,1)} async-done(((bf16[512,2048]{1,0:T(8,128)(2,1)}), bf16[2048,2048]{1,0:T(8,128)(2,1)}) %all-gather.5.cloned.1.call-update) | async-done | bytes 8388624 | tf_op jit(solution)/shard_map/all_gather | solution.py:85
  148.6 14.2 %fusion.6 = f32[2048,896]{1,0:T(8,128)} fusion(bf16[2048,2048]{1,0:T(8,128)(2,1)} %all-gather.5.cloned.1.call-done, bf16[1,896,2048]{2,1,0:T(8,128)(2,1)} %param.15), kind=kOutput, calls=%fused_computation.8 | convolution fusion | flops 7516192768 | bytes 19398656 | tf_op jit(solution)/shard_map/dot_general | solution.py:13
  162.8 26.7 %fusion.2 = f32[2048,2048]{1,0:T(8,128)} fusion(f32[2048,896]{1,0:T(8,128)} %fusion.6, bf16[2048,2048]{1,0:T(8,128)(2,1)} %all-gather.5.cloned.1.call-done, bf16[1,896,2048]{2,1,0:T(8,128)(2,1)} %param.17, bf16[1,896,2048]{2,1,0:T(8,128)(2,1)} %param.16), kind=kOutput, calls=%fused_computation.5 | convolution fusion | flops 15043395584 | bytes 39845888 | tf_op jit(solution)/shard_map/dot_general | solution.py:20
  189.5 0.0 reduce-scatter.2.cloned.1.call-update
  189.5 153.9 %reduce-scatter.2.cloned.1.call-done = f32[512,2048]{1,0:T(8,128)} async-done(((f32[2048,2048]{1,0:T(8,128)}), f32[512,2048]{1,0:T(8,128)}) %reduce-scatter.2.cloned.1.call-update) | async-done | bytes 4194320 | tf_op jit(solution)/shard_map/reduce_scatter | solution.py:86
  343.4 5.0 %all-to-all-start.1 = ((f32[4,128,2048]{2,1,0:T(8,128)}), f32[4,128,2048]{2,1,0:T(8,128)}, u32[]{:S(2)}, u32[]{:S(2)}) async-start(f32[4,128,2048]{2,1,0:T(8,128)} %bitcast.61), calls=%async_computation.2 | async-start | bytes 8388608 | tf_op jit(solution)/shard_map/all_to_all | solution.py:92
  348.4 0.0 copy-start.3
  348.4 0.0 copy-start.5
  348.4 0.3 all-reduce.2.cloned.1.call-start
  348.7 0.1 select_reduce_fusion
  348.8 92.9 %all-to-all-done.1 = f32[4,128,2048]{2,1,0:T(8,128)} async-done(((f32[4,128,2048]{2,1,0:T(8,128)}), f32[4,128,2048]{2,1,0:T(8,128)}, u32[]{:S(2)}, u32[]{:S(2)}) %all-to-all-start.1) | async-done | bytes 4194336 | tf_op jit(solution)/shard_map/all_to_all | solution.py:92
  441.7 4.6 fusion.34
  446.3 1.3 fusion.35
  447.5 0.0 all-reduce.2.cloned.1.call-update
  447.6 0.1 slice_bitcast_fusion.1
  447.6 0.1 copy.39
  447.8 0.2 reduce-window.19
  447.9 0.1 reduce.1
  448.0 15.5 %all-reduce.2.cloned.1.call-done = f32[128,128]{1,0:T(8,128)} async-done(((f32[128,128]{1,0:T(8,128)}), f32[128,128]{1,0:T(8,128)}) %all-reduce.2.cloned.1.call-update) | async-done | bytes 65552 | tf_op jit(solution)/shard_map/psum | solution.py:113
  463.6 1.0 select_reduce_fusion.1
  464.6 0.1 slice_bitcast_fusion
  464.6 0.8 convolution_bitcast_fusion
  465.5 1.5 copy.43
  (16 shorter events, 0.1 us)
Async XLA Ops:
  7.2 439.1 %copy-start = (bf16[2048,128]{1,0:T(8,128)(2,1)S(1)}, bf16[2048,128]{1,0:T(8,128)(2,1)}, u32[]{:S(2)}) copy-start(bf16[2048,128]{1,0:T(8,128)(2,1)} %param.18) | copy-start | bytes 1572868
  7.2 37.2 %copy-start.1 = (bf16[2048]{0:T(1024)(128)(2,1)S(1)}, bf16[2048]{0:T(1024)(128)(2,1)}, u32[]{:S(2)}) copy-start(bf16[2048]{0:T(1024)(128)(2,1)} %param.12) | copy-start | bytes 12292
  7.2 47.0 %all-gather.3.cloned.1.call-start = ((), (), s32[]{:S(2)}) async-start(), calls=%async_computation.3 | async-start | bytes 3145728 | tf_op jit(solution)/shard_map/all_gather | solution.py:79
  44.4 104.2 %all-gather.5.cloned.1.call-start = ((), (), s32[]{:S(2)}) async-start(), calls=%async_computation.4 | async-start | bytes 10485760 | tf_op jit(solution)/shard_map/all_gather | solution.py:85
  59.7 283.6 %reduce-scatter.2.cloned.1.call-start = ((), (), s32[]{:S(2)}) async-start(), calls=%async_computation.5 | async-start | bytes 20971520 | tf_op jit(solution)/shard_map/reduce_scatter | solution.py:86
  343.4 5.3 %copy-start.2 = (s32[128,2]{0,1:T(2,128)S(1)}, s32[128,2]{0,1:T(2,128)}, u32[]{:S(2)}) copy-start(s32[128,2]{0,1:T(2,128)} %param.14) | copy-start | bytes 3076
  343.4 5.4 %copy-start.4 = (s32[128]{0:T(128)S(1)}, s32[128]{0:T(128)}, u32[]{:S(2)}) copy-start(s32[128]{0:T(128)} %param.21) | copy-start | bytes 1540
  343.4 98.3 %all-to-all-start.1 = ((f32[4,128,2048]{2,1,0:T(8,128)}), f32[4,128,2048]{2,1,0:T(8,128)}, u32[]{:S(2)}, u32[]{:S(2)}) async-start(f32[4,128,2048]{2,1,0:T(8,128)} %bitcast.61), calls=%async_computation.2 | async-start | bytes 8388608 | tf_op jit(solution)/shard_map/all_to_all | solution.py:92
  348.4 115.2 %copy-start.3 = (s32[128]{0:T(128)S(1)}, s32[128]{0:T(128)}, u32[]{:S(2)}) copy-start(s32[128]{0:T(128)} %param.19) | copy-start | bytes 1540
  348.4 116.2 %copy-start.5 = (s32[128]{0:T(128)S(1)}, s32[128]{0:T(128)}, u32[]{:S(2)}) copy-start(s32[128]{0:T(128)} %param.20) | copy-start | bytes 1540
  348.4 115.1 %all-reduce.2.cloned.1.call-start = ((), (), s32[]{:S(2)}) async-start(), calls=%async_computation.6 | async-start | bytes 131072 | tf_op jit(solution)/shard_map/psum | solution.py:113
Sparse Core Ops, SparseCore 0:
  44.5 9.6 all-gather.2
  59.9 88.6 all-gather.4
  189.6 153.7 reduce-scatter.1
  447.7 15.8 all-reduce.1
where the time goes:
time: 474 us; the launch traced here: 473 us
  waiting for transfers between devices  361 us (76%)
  matrix products  48.9 us (10%)
  blocking collectives  32 us (7%)
  between operations  13.9 us (3%)
  other arithmetic  9.03 us (2%)
  starting transfers between devices  5.55 us (1%)
    reduce_scatter x1, waiting for transfers between devices, per_device(): lax.psum_scatter(expert_rows(gathered, gate_weights[0], up_weights[0], do...  154 us
    all_to_all x1, waiting for transfers between devices, per_device(): lax.all_to_all(payload.reshape(groups, capacity, payload.shape[1]), 'expe...  92.9 us
    all_gather x1, waiting for transfers between devices, per_device(): gathered = lax.all_gather(normed, 'dp', axis=0, tiled=True)  88.6 us
    all_to_all x1, blocking collectives, per_device(): lax.all_to_all(outgoing, 'expert', split_axis=0, concat_axis=0, tiled=True)  32 us
    dot_general x1, matrix products, expert_rows(): return jnp.dot(hidden, down_matrix, preferred_element_type=jnp.float32)  26.7 us
    psum x1, waiting for transfers between devices, per_device(): action_values = lax.psum(partial_values, 'tensor')  15.5 us
    dot_general x1, matrix products, expert_rows(): lax.dot_general(row_block, gate_matrix, (((1,), (1,)), ((), ())), preferr...  14.2 us
    all_gather x1, waiting for transfers between devices, per_device(): arrived = lax.all_gather(arrived, 'tensor', axis=2, tiled=True)  9.76 us
  transfers between devices with their start and end apart: 5, of which 5 were waited for; matrix products, arithmetic and copies ran while one was open for 0% of the time, Pallas kernels for 0%

commit v1 on v0

--- a/solution.py
+++ b/solution.py
@@ -82,7 +82,9 @@
     widened = row_block.astype(jnp.float32)
     scaling = lax.rsqrt(jnp.mean(widened * widened, axis=1, keepdims=True) + EPSILON)
     normed = (widened * scaling * norm_gain.astype(jnp.float32)[None, :]).astype(jnp.bfloat16)
-    gathered = lax.all_gather(normed, "dp", axis=0, tiled=True)
+    gathered = jnp.concatenate(
+        lax.all_to_all(jnp.stack([normed] * lax.axis_size("dp")), "dp", 0, 0), axis=0
+    )
     payload = lax.psum_scatter(
         expert_rows(gathered, gate_weights[0], up_weights[0], down_weights[0]),
         "dp",

time: 474 us -> 482 us (1.017)
  blocking collectives: 32 us -> 129 us
  waiting for transfers between devices: 361 us -> 272 us
    all_to_all x0 -> x1, blocking collectives: none -> 97.2 us  [per_device(): lax.all_to_all(jnp.stack([normed] * lax.axis_size('dp')), 'dp', 0, 0)]
    all_gather x1 -> x0, waiting for transfers between devices: 88.6 us -> none  [per_device(): gathered = lax.all_gather(normed, 'dp', axis=0, tiled=True)]
  transfers between devices with their start and end apart: 5 -> 4, of which waited for: 5 -> 4; matrix products, arithmetic and copies ran while one was open for 0% -> 0% of each run, Pallas kernels for 0% -> 0%
where the time goes in v1:
time: 482 us; the launch traced here: 481 us
  waiting for transfers between devices  272 us (56%)
  blocking collectives  129 us (27%)
  matrix products  45.6 us (9%)
  between operations  13.9 us (3%)
  other arithmetic  7.73 us (2%)
  local copies, waits for them, and re-layouts  7.66 us (2%)
  starting transfers between devices  5.33 us (1%)
    reduce_scatter x1, waiting for transfers between devices, per_device(): lax.psum_scatter(expert_rows(gathered, gate_weights[0], up_weights[0], do...  153 us
    all_to_all x1, blocking collectives, per_device(): lax.all_to_all(jnp.stack([normed] * lax.axis_size('dp')), 'dp', 0, 0)  97.2 us
    all_to_all x1, waiting for transfers between devices, per_device(): lax.all_to_all(payload.reshape(groups, capacity, payload.shape[1]), 'expe...  92.9 us
    all_to_all x1, blocking collectives, per_device(): lax.all_to_all(outgoing, 'expert', split_axis=0, concat_axis=0, tiled=True)  32 us
    dot_general x1, matrix products, expert_rows(): return jnp.dot(hidden, down_matrix, preferred_element_type=jnp.float32)  26.7 us
    psum x1, waiting for transfers between devices, per_device(): action_values = lax.psum(partial_values, 'tensor')  15.6 us
    dot_general x1, matrix products, expert_rows(): lax.dot_general(row_block, gate_matrix, (((1,), (1,)), ((), ())), preferr...  10.9 us
    all_gather x1, waiting for transfers between devices, per_device(): arrived = lax.all_gather(arrived, 'tensor', axis=2, tiled=True)  9.76 us
  transfers between devices with their start and end apart: 4, of which 4 were waited for; matrix products, arithmetic and copies ran while one was open for 0% of the time, Pallas kernels for 0%

profile of v1, /device:TPU:0, one launch (start us, length us, event | category | flops | bytes accessed | tf_op | source)
XLA Modules:
  0.0 481.0 jit_solution(4002318857393006773)
XLA Ops:
  7.2 0.0 copy-start
  7.2 0.0 copy-start.2
  7.2 0.0 all-gather.2.cloned.1.call-start
  7.2 0.8 copy.34
  8.1 0.1 eq.53
  8.2 0.1 eq.49
  8.4 1.2 reduce-window.14
  9.6 0.1 slice.20
  9.7 0.1 copy.36
  9.8 0.1 copy.37
  9.9 0.1 add_bitcast_fusion
  10.0 0.1 reduce_sum.48
  10.2 0.1 copy.38
  10.2 0.7 multiply_add_fusion
  10.9 0.1 fusion.9
  11.0 1.4 convolution_convert_fusion
  12.4 32.0 %all_to_all.15 = bf16[4,128,1024]{2,1,0:T(8,128)(2,1)} all-to-all(bf16[4,128,1024]{2,1,0:T(8,128)(2,1)S(1)} %bitcast.65), channel_id=1, replica_groups=mesh['dp'=4,'expert'=4,'tensor'=2] {'expert'}, dimensions={0} | all-to-all | bytes 2097152 | tf_op jit(solution)/shard_map/all_to_all | solution.py:78
  44.3 0.0 all-gather.2.cloned.1.call-update
  44.4 0.0 reduce-scatter.2.cloned.1.call-start
  44.4 9.8 %all-gather.2.cloned.1.call-done = bf16[4,128,2048]{2,1,0:T(8,128)(2,1)} async-done(((bf16[4,128,1024]{2,1,0:T(8,128)(2,1)}), bf16[4,128,2048]{2,1,0:T(8,128)(2,1)}) %all-gather.2.cloned.1.call-update) | async-done | bytes 2097168 | tf_op jit(solution)/shard_map/all_gather | solution.py:79
  54.2 2.1 multiply_reduce_fusion
  56.3 2.1 fusion.1
  58.4 1.1 stack.2
  59.5 0.0 copy-start.5
  59.5 97.2 %all_to_all.16 = bf16[4,512,2048]{2,1,0:T(8,128)(2,1)S(1)} all-to-all(bf16[4,512,2048]{2,1,0:T(8,128)(2,1)S(1)} %stack.2), channel_id=1, replica_groups=mesh['dp'=4,'expert'=4,'tensor'=2] {'dp'}, dimensions={0} | all-to-all | bytes 16777216 | tf_op jit(solution)/shard_map/all_to_all | solution.py:86
  156.8 3.2 copy-done.1
  160.0 10.9 %fusion.6 = f32[2048,896]{1,0:T(8,128)} fusion(bf16[2048,2048]{1,0:T(8,128)(2,1)S(1)} %bitcast.62, bf16[1,896,2048]{2,1,0:T(8,128)(2,1)S(1)} %copy-done.5), kind=kOutput, calls=%fused_computation.8 | convolution fusion | flops 7516192768 | bytes 19398656 | tf_op jit(solution)/shard_map/dot_general | solution.py:13
  170.9 26.7 %fusion.2 = f32[2048,2048]{1,0:T(8,128)} fusion(f32[2048,896]{1,0:T(8,128)} %fusion.6, bf16[2048,2048]{1,0:T(8,128)(2,1)} %bitcast.63, bf16[1,896,2048]{2,1,0:T(8,128)(2,1)} %param.17, bf16[1,896,2048]{2,1,0:T(8,128)(2,1)} %param.16), kind=kOutput, calls=%fused_computation.5 | convolution fusion | flops 15043395584 | bytes 39845888 | tf_op jit(solution)/shard_map/dot_general | solution.py:20
  197.6 0.0 reduce-scatter.2.cloned.1.call-update
  197.6 153.3 %reduce-scatter.2.cloned.1.call-done = f32[512,2048]{1,0:T(8,128)} async-done(((f32[2048,2048]{1,0:T(8,128)}), f32[512,2048]{1,0:T(8,128)}) %reduce-scatter.2.cloned.1.call-update) | async-done | bytes 4194320 | tf_op jit(solution)/shard_map/reduce_scatter | solution.py:88
  350.9 5.0 %all-to-all-start.2 = ((f32[4,128,2048]{2,1,0:T(8,128)}), f32[4,128,2048]{2,1,0:T(8,128)}, u32[]{:S(2)}, u32[]{:S(2)}) async-start(f32[4,128,2048]{2,1,0:T(8,128)} %bitcast.64), calls=%async_computation.3 | async-start | bytes 8388608 | tf_op jit(solution)/shard_map/all_to_all | solution.py:94
  355.9 0.0 copy-start.4
  355.9 0.0 copy-start.7
  356.0 0.3 all-reduce.2.cloned.1.call-start
  356.3 0.1 select_reduce_fusion
  356.4 92.9 %all-to-all-done.2 = f32[4,128,2048]{2,1,0:T(8,128)} async-done(((f32[4,128,2048]{2,1,0:T(8,128)}), f32[4,128,2048]{2,1,0:T(8,128)}, u32[]{:S(2)}, u32[]{:S(2)}) %all-to-all-start.2) | async-done | bytes 4194336 | tf_op jit(solution)/shard_map/all_to_all | solution.py:94
  449.3 4.5 fusion.34
  453.8 1.3 fusion.35
  455.0 0.0 all-reduce.2.cloned.1.call-update
  455.1 0.1 slice_bitcast_fusion.1
  455.1 0.1 copy.39
  455.3 0.2 reduce-window.19
  455.4 0.1 reduce.1
  455.5 15.6 %all-reduce.2.cloned.1.call-done = f32[128,128]{1,0:T(8,128)} async-done(((f32[128,128]{1,0:T(8,128)}), f32[128,128]{1,0:T(8,128)}) %all-reduce.2.cloned.1.call-update) | async-done | bytes 65552 | tf_op jit(solution)/shard_map/psum | solution.py:115
  471.1 1.0 select_reduce_fusion.1
  472.1 0.1 slice_bitcast_fusion
  472.2 0.8 convolution_bitcast_fusion
  473.0 1.5 copy.43
  (19 shorter events, 0.1 us)
Async XLA Ops:
  7.2 446.6 %copy-start = (bf16[2048,128]{1,0:T(8,128)(2,1)S(1)}, bf16[2048,128]{1,0:T(8,128)(2,1)}, u32[]{:S(2)}) copy-start(bf16[2048,128]{1,0:T(8,128)(2,1)} %param.18) | copy-start | bytes 1572868
  7.2 37.2 %copy-start.2 = (bf16[2048]{0:T(1024)(128)(2,1)S(1)}, bf16[2048]{0:T(1024)(128)(2,1)}, u32[]{:S(2)}) copy-start(bf16[2048]{0:T(1024)(128)(2,1)} %param.12) | copy-start | bytes 12292
  7.2 47.0 %all-gather.2.cloned.1.call-start = ((), (), s32[]{:S(2)}) async-start(), calls=%async_computation.4 | async-start | bytes 3145728 | tf_op jit(solution)/shard_map/all_gather | solution.py:79
  44.4 306.6 %reduce-scatter.2.cloned.1.call-start = ((), (), s32[]{:S(2)}) async-start(), calls=%async_computation.5 | async-start | bytes 20971520 | tf_op jit(solution)/shard_map/reduce_scatter | solution.py:88
  59.5 100.5 %copy-start.5 = (bf16[1,896,2048]{2,1,0:T(8,128)(2,1)S(1)}, bf16[1,896,2048]{2,1,0:T(8,128)(2,1)}, u32[]{:S(2)}) copy-start(bf16[1,896,2048]{2,1,0:T(8,128)(2,1)} %param.15) | copy-start | bytes 11010052
  156.8 3.2 copy-start.1
  350.9 5.3 %copy-start.3 = (s32[128,2]{0,1:T(2,128)S(1)}, s32[128,2]{0,1:T(2,128)}, u32[]{:S(2)}) copy-start(s32[128,2]{0,1:T(2,128)} %param.14) | copy-start | bytes 3076
  350.9 5.4 %copy-start.6 = (s32[128]{0:T(128)S(1)}, s32[128]{0:T(128)}, u32[]{:S(2)}) copy-start(s32[128]{0:T(128)} %param.21) | copy-start | bytes 1540
  350.9 98.3 %all-to-all-start.2 = ((f32[4,128,2048]{2,1,0:T(8,128)}), f32[4,128,2048]{2,1,0:T(8,128)}, u32[]{:S(2)}, u32[]{:S(2)}) async-start(f32[4,128,2048]{2,1,0:T(8,128)} %bitcast.64), calls=%async_computation.3 | async-start | bytes 8388608 | tf_op jit(solution)/shard_map/all_to_all | solution.py:94
  355.9 115.2 %copy-start.4 = (s32[128]{0:T(128)S(1)}, s32[128]{0:T(128)}, u32[]{:S(2)}) copy-start(s32[128]{0:T(128)} %param.19) | copy-start | bytes 1540
  355.9 116.2 %copy-start.7 = (s32[128]{0:T(128)S(1)}, s32[128]{0:T(128)}, u32[]{:S(2)}) copy-start(s32[128]{0:T(128)} %param.20) | copy-start | bytes 1540
  356.0 115.1 %all-reduce.2.cloned.1.call-start = ((), (), s32[]{:S(2)}) async-start(), calls=%async_computation.6 | async-start | bytes 131072 | tf_op jit(solution)/shard_map/psum | solution.py:115
Sparse Core Ops, SparseCore 0:
  44.5 9.6 all-gather.1
  197.7 153.1 reduce-scatter.1
  455.2 15.8 all-reduce.1
